TPU v7x, 32 devices: a whole 2x2x4 slice. The times are simulated.
32 devices in a mesh: groups: 2 (over x), shard: 16 (over z, y, core).
Axes of the slice: x: 2, y: 2, z: 4, core: 2. Of those that a mesh axis runs over, the one named last changes fastest.
Arguments:
- embeddings: bfloat16 [16384, 1024], P(('groups', 'shard')), parts along dimension 0, may hold values from -6 to 6
- scales: bfloat16 [16384], P(('groups', 'shard')), parts along dimension 0, may hold values from 0.039794922 to 0.119628906
- cluster: int32 [16384, 1], P(('groups', 'shard')), parts along dimension 0, may hold values from 0 to 15; in each aligned block of 512 rows (0 to 511, 512 to 1023, ...) at most 64 rows name the same one
- pair_listed: int32 [32, 5], P(('groups', 'shard')), parts along dimension 0, may hold values from 0 to 1, as said below
Outputs:
- best: float32 [16384], P(('groups', 'shard')), parts along dimension 0
There are 2 independent parts, one for each index of `groups`. A program takes and returns all parts, laid end to end along the dimension named above; each array names one. Nothing has to cross between parts.
Inputs may be any that keep to these rules, and one draw needn't show every extreme that they name: In each shard's 512 rows at most 64 rows name one sub-cluster, and every sub-cluster is named by some row of the group. `pair_listed`: column 0 is 1 for every a < 15; entries with a + k + 1 >= 16 are 0.
All inputs are finite; a program needn't handle non-finite values.
Results may differ from a plain program's by a relative error of at most 0.0003.
Values may be sent and summed in bfloat16 or wider, within the bound.
A program may use at most 64 MiB of HBM per device.

v0:
```python
import jax
import jax.numpy as jnp
from jax import lax
from jax.sharding import PartitionSpec as P

PARTNERS = 5


lowest = -jnp.inf


def passed_along(value, axis, steps):
    count = lax.axis_size(axis)
    initial, last = (max(0, -steps), min(count, count - steps))
    return lax.ppermute(value, axis, [(source, source + steps) for source in range(initial, last)])


def scaled_tile(left, left_scale, right, right_scale):
    raw = lax.dot_general(left, right, (((1,), (1,)), ((), ())), preferred_element_type=jnp.float32)
    return raw * left_scale.astype(jnp.float32)[:, None] * right_scale.astype(jnp.float32)[None, :]


def partner_tile(left, left_scale, right, right_scale):
    scores = scaled_tile(left, left_scale, right, right_scale)
    live = (left_scale != 0)[:, None] & (right_scale != 0)[None, :]
    masked = jnp.where(live, scores, lowest)
    return (jnp.max(masked, axis=1), jnp.max(masked, axis=0))


def per_device(embeddings, scales, cluster, pair_listed):
    rows, width = embeddings.shape
    owners = lax.axis_size("shard")
    capacity = 2 * rows // owners
    slots = owners * capacity
    here = lax.axis_index("shard")
    target = cluster[:, 0]
    onehot = (target[:, None] == jnp.arange(owners, dtype=jnp.int32)[None, :]).astype(jnp.int32)
    before = jnp.cumsum(onehot, axis=0) - onehot
    position = target * capacity + jnp.sum(before * onehot, axis=1)
    placing = (jnp.arange(slots, dtype=jnp.int32)[:, None] == position[None, :]).astype(
        jnp.bfloat16
    )
    packed = jnp.dot(placing, embeddings, preferred_element_type=jnp.float32).astype(jnp.bfloat16)
    packed_scale = jnp.dot(placing, scales, preferred_element_type=jnp.float32).astype(jnp.bfloat16)
    block, block_scale = (
        lax.all_to_all(
            packed.reshape(owners, capacity, width),
            "shard",
            split_axis=0,
            concat_axis=0,
            tiled=True,
        ),
        lax.all_to_all(
            packed_scale.reshape(owners, capacity), "shard", split_axis=0, concat_axis=0, tiled=True
        ),
    )
    block = block.reshape(slots, width)
    block_scale = block_scale.reshape(slots)
    valid = block_scale != 0
    scores = scaled_tile(block, block_scale, block, block_scale)
    counter = jnp.arange(slots, dtype=jnp.int32)
    keep = valid[None, :] & (counter[:, None] != counter[None, :])
    row_best = jnp.max(jnp.where(keep, scores, lowest), axis=1)
    column_best = []
    carried = (block, block_scale)
    for step in range(PARTNERS):
        carried = passed_along((carried[0], carried[1]), "shard", -1)
        listed = pair_listed[0, step] == 1
        rows_part, cols_part = partner_tile(block, block_scale, carried[0], carried[1])
        rows_part = jnp.where(listed, rows_part, lowest)
        cols_part = jnp.where(listed, cols_part, lowest)
        row_best = jnp.maximum(row_best, rows_part)
        column_best.append(cols_part)
    returned = column_best[PARTNERS - 1]
    for step in range(PARTNERS - 1, -1, -1):
        returned = passed_along(returned, "shard", 1)
        returned = jnp.where(here == 0, lowest, returned)
        if step > 0:
            returned = jnp.maximum(returned, column_best[step - 1])
    slot_best = jnp.where(valid, jnp.maximum(row_best, returned), 0.0)
    homeward = lax.all_to_all(
        slot_best.reshape(owners, capacity), "shard", split_axis=0, concat_axis=0, tiled=True
    )
    return jnp.take(homeward.reshape(slots), position)


def solution(mesh):
    placed = (
        P(("groups", "shard"), None),
        P(("groups", "shard")),
        P(("groups", "shard"), None),
        P(("groups", "shard"), None),
    )
    return jax.shard_map(
        per_device, mesh=mesh, in_specs=placed, out_specs=P(("groups", "shard")), check_vma=False
    )
```

profile of v0, /device:TPU:0, one launch (start us, length us, event | category | flops | bytes accessed | tf_op | source)
XLA Modules:
  0.0 281.8 jit_solution(17017823350575949528)
XLA Ops:
  4.9 54.4 %all_to_all.24 = bf16[16,64,1024]{2,1,0:T(8,128)(2,1)S(1)} all-to-all(bf16[16,64,1024]{2,1,0:T(8,128)(2,1)S(1)} %bitcast.52), channel_id=1, replica_groups=mesh['groups'=2,'shard'=16] {'shard'}, dimensions={0} | all-to-all | bytes 4194304 | tf_op jit(solution)/shard_map/all_to_all | solution.py:46
  60.6 5.2 %collective-permute-done.1 = bf16[1024,1024]{1,0:T(8,128)(2,1)S(1)} collective-permute-done((bf16[1024,1024]{1,0:T(8,128)(2,1)S(1)}, bf16[1024,1024]{1,0:T(8,128)(2,1)S(1)}, u32[]{:S(2)}, u32[]{:S(2)}) %collective-permute-start.1) | collective-permute-done | bytes 2097184 | tf_op jit(solution)/shard_map/ppermute | solution.py:15
  67.1 26.1 %collective-permute-done.3 = bf16[1024,1024]{1,0:T(8,128)(2,1)S(1)} collective-permute-done((bf16[1024,1024]{1,0:T(8,128)(2,1)S(1)}, bf16[1024,1024]{1,0:T(8,128)(2,1)S(1)}, u32[]{:S(2)}, u32[]{:S(2)}) %collective-permute-start.3) | collective-permute-done | bytes 2097184 | tf_op jit(solution)/shard_map/ppermute | solution.py:15
  94.4 26.2 %collective-permute-done.5 = bf16[1024,1024]{1,0:T(8,128)(2,1)} collective-permute-done((bf16[1024,1024]{1,0:T(8,128)(2,1)S(1)}, bf16[1024,1024]{1,0:T(8,128)(2,1)}, u32[]{:S(2)}, u32[]{:S(2)}) %collective-permute-start.5) | collective-permute-done | bytes 2097184 | tf_op jit(solution)/shard_map/ppermute | solution.py:15
  123.1 29.6 %all-to-all-start = ((bf16[16,1,64]{2,1,0:T(2,128)(2,1)}), bf16[16,1,64]{2,1,0:T(2,128)(2,1)S(1)}, u32[]{:S(2)}, u32[]{:S(2)}) async-start(bf16[16,1,64]{2,1,0:T(2,128)(2,1)} %all_to_all.20), calls=%async_computation | async-start | bytes 16384 | tf_op jit(solution)/shard_map/all_to_all | solution.py:53
  154.1 20.4 %all-to-all-done = bf16[16,1,64]{2,1,0:T(2,128)(2,1)S(1)} async-done(((bf16[16,1,64]{2,1,0:T(2,128)(2,1)}), bf16[16,1,64]{2,1,0:T(2,128)(2,1)S(1)}, u32[]{:S(2)}, u32[]{:S(2)}) %all-to-all-start) | async-done | bytes 2080 | tf_op jit(solution)/shard_map/all_to_all | solution.py:53
  179.0 2.9 %collective-permute-done.2 = bf16[1024]{0:T(1024)(128)(2,1)S(1)} collective-permute-done((bf16[1024]{0:T(1024)(128)(2,1)S(1)}, bf16[1024]{0:T(1024)(128)(2,1)S(1)}, u32[]{:S(2)}, u32[]{:S(2)}) %collective-permute-start.2) | collective-permute-done | bytes 2080 | tf_op jit(solution)/shard_map/ppermute | solution.py:15
  183.2 3.6 %collective-permute-done.4 = bf16[1024]{0:T(1024)(128)(2,1)S(1)} collective-permute-done((bf16[1024]{0:T(1024)(128)(2,1)S(1)}, bf16[1024]{0:T(1024)(128)(2,1)S(1)}, u32[]{:S(2)}, u32[]{:S(2)}) %collective-permute-start.4) | collective-permute-done | bytes 2080 | tf_op jit(solution)/shard_map/ppermute | solution.py:15
  188.1 3.6 %collective-permute-done.6 = bf16[1024]{0:T(1024)(128)(2,1)S(1)} collective-permute-done((bf16[1024]{0:T(1024)(128)(2,1)S(1)}, bf16[1024]{0:T(1024)(128)(2,1)S(1)}, u32[]{:S(2)}, u32[]{:S(2)}) %collective-permute-start.6) | collective-permute-done | bytes 2080 | tf_op jit(solution)/shard_map/ppermute | solution.py:15
  193.0 3.6 %collective-permute-done.8 = bf16[1024]{0:T(1024)(128)(2,1)S(1)} collective-permute-done((bf16[1024]{0:T(1024)(128)(2,1)S(1)}, bf16[1024]{0:T(1024)(128)(2,1)S(1)}, u32[]{:S(2)}, u32[]{:S(2)}) %collective-permute-start.8) | collective-permute-done | bytes 2080 | tf_op jit(solution)/shard_map/ppermute | solution.py:15
  198.2 4.0 %fusion.21 = f32[1024,1024]{0,1:T(8,128)S(1)} fusion(bf16[1024,1024]{1,0:T(8,128)(2,1)S(1)} %bitcast.46, bf16[1024,1024]{1,0:T(8,128)(2,1)} %copy-done.4), kind=kOutput, calls=%fused_computation.52 | convolution fusion | flops 2147483648 | bytes 8388608 | tf_op jit(solution)/shard_map/dot_general | solution.py:19
  202.2 2.4 fusion.22
  204.7 4.0 %fusion.23 = f32[1024,1024]{0,1:T(8,128)S(1)} fusion(bf16[1024,1024]{1,0:T(8,128)(2,1)S(1)} %bitcast.48, bf16[1024,1024]{1,0:T(8,128)(2,1)} %collective-permute-done.5), kind=kOutput, calls=%fused_computation.54 | convolution fusion | flops 2147483648 | bytes 8388608 | tf_op jit(solution)/shard_map/dot_general | solution.py:19
  208.6 4.0 %fusion.24 = f32[1024,1024]{0,1:T(8,128)S(1)} fusion(bf16[1024,1024]{1,0:T(8,128)(2,1)S(1)} %bitcast.49, bf16[1024,1024]{1,0:T(8,128)(2,1)} %collective-permute-done.7), kind=kOutput, calls=%fused_computation.55 | convolution fusion | flops 2147483648 | bytes 8388608 | tf_op jit(solution)/shard_map/dot_general | solution.py:19
  212.6 8.0 %fusion.2 = (f32[1024]{0:T(1024)S(1)}, f32[1024]{0:T(1024)S(1)}, f32[1024]{0:T(1024)S(1)}, f32[1024]{0:T(1024)S(1)}, f32[1024]{0:T(1024)S(1)}, /*index=5*/f32[10...) fusion(f32[1024,1024]{0,1:T(8,128)S(1)} %fusion.21, ...), kind=kOutput, calls=%fused_computation.10 | convolution fusion | flops 2178930688 | bytes 21043200 | tf_op jit(solution)/shard_map/dot_general | solution.py:19
  220.6 17.0 %collective-permute-start.10 = (f32[1024]{0:T(1024)S(1)}, f32[1024]{0:T(1024)S(1)}, u32[]{:S(2)}, u32[]{:S(2)}) collective-permute-start(f32[1024]{0:T(1024)S(1)} %broadcast_select_fusion), channel_id=1, source_target_pairs={{0,1},{1,2},{2,3},{3,4},{4,5},{5,6},{6,7},{7,8},{8,9},{9,10},{10,1... | collective-permute-start | bytes 12296 | tf_op jit(solution)/shard_map/ppermute | solution.py:15
  238.5 2.2 collective-permute-start.11
  241.5 7.3 %collective-permute-start.12 = (f32[1024]{0:T(1024)S(1)}, f32[1024]{0:T(1024)S(1)}, u32[]{:S(2)}, u32[]{:S(2)}) collective-permute-start(f32[1024]{0:T(1024)S(1)} %select_maximum_fusion.2), channel_id=1, source_target_pairs={{0,1},{1,2},{2,3},{3,4},{4,5},{5,6},{6,7},{7,8},{8,9},{9,10},{10,1... | collective-permute-start | bytes 12296 | tf_op jit(solution)/shard_map/ppermute | solution.py:15
  249.7 4.1 %collective-permute-start.13 = (f32[1024]{0:T(1024)S(1)}, f32[1024]{0:T(1024)S(1)}, u32[]{:S(2)}, u32[]{:S(2)}) collective-permute-start(f32[1024]{0:T(1024)S(1)} %select_maximum_fusion.1), channel_id=1, source_target_pairs={{0,1},{1,2},{2,3},{3,4},{4,5},{5,6},{6,7},{7,8},{8,9},{9,10},{10,1... | collective-permute-start | bytes 12296 | tf_op jit(solution)/shard_map/ppermute | solution.py:15
  254.6 4.1 %collective-permute-start.14 = (f32[1024]{0:T(1024)S(1)}, f32[1024]{0:T(1024)S(1)}, u32[]{:S(2)}, u32[]{:S(2)}) collective-permute-start(f32[1024]{0:T(1024)S(1)} %select_maximum_fusion), channel_id=1, source_target_pairs={{0,1},{1,2},{2,3},{3,4},{4,5},{5,6},{6,7},{7,8},{8,9},{9,10},{10,1... | collective-permute-start | bytes 12296 | tf_op jit(solution)/shard_map/ppermute | solution.py:15
  258.7 2.5 select_reduce_fusion
  261.9 9.3 %all-to-all-start.2 = ((f32[16,1,64]{2,1,0:T(1,128)}), f32[16,1,64]{2,1,0:T(1,128)S(1)}, u32[]{:S(2)}, u32[]{:S(2)}) async-start(f32[16,1,64]{2,1,0:T(1,128)} %all_to_all.18), calls=%async_computation.2 | async-start | bytes 16384 | tf_op jit(solution)/shard_map/all_to_all | solution.py:81
  271.2 6.4 %all-to-all-done.2 = f32[16,1,64]{2,1,0:T(1,128)S(1)} async-done(((f32[16,1,64]{2,1,0:T(1,128)}), f32[16,1,64]{2,1,0:T(1,128)S(1)}, u32[]{:S(2)}, u32[]{:S(2)}) %all-to-all-start.2) | async-done | bytes 4128 | tf_op jit(solution)/shard_map/all_to_all | solution.py:81
  278.9 2.3 gather_fusion
  (72 shorter events, 25.1 us)
Async XLA Ops:
  0.0 3.6 %copy-start = (bf16[512,1024]{1,0:T(8,128)(2,1)S(1)}, bf16[512,1024]{1,0:T(8,128)(2,1)}, u32[]{:S(2)}) copy-start(bf16[512,1024]{1,0:T(8,128)(2,1)} %param.4) | copy-start | bytes 3145732
  4.9 117.0 %copy-start.3 = (bf16[512]{0:T(512)(128)(2,1)S(1)}, bf16[512]{0:T(512)(128)(2,1)}, u32[]{:S(2)}) copy-start(bf16[512]{0:T(512)(128)(2,1)} %param.5) | copy-start | bytes 3076
  4.9 147.8 %copy-start.2 = (s32[1,5]{1,0:T(1,128)S(1)}, s32[1,5]{1,0:T(1,128)}, u32[]{:S(2)}) copy-start(s32[1,5]{1,0:T(1,128)} %param.7) | copy-start | bytes 64
  59.3 6.5 %collective-permute-start.1 = (bf16[1024,1024]{1,0:T(8,128)(2,1)S(1)}, bf16[1024,1024]{1,0:T(8,128)(2,1)S(1)}, u32[]{:S(2)}, u32[]{:S(2)}) collective-permute-start(bf16[1024,1024]{1,0:T(8,128)(2,1)S(1)} %bitcast.45), channel_id=1, source_target_pairs={{1,0},{2,1},{3,2},{4,3},{5,4},{6,5},{7,6},{8,7},{9,8},{10,9},{11,1... | collective-permute-start | bytes 6291464 | tf_op jit(solution)/shard_map/ppermute | solution.py:15
  65.8 54.8 %copy-start.4 = (bf16[1024,1024]{1,0:T(8,128)(2,1)}, bf16[1024,1024]{1,0:T(8,128)(2,1)S(1)}, u32[]{:S(2)}) copy-start(bf16[1024,1024]{1,0:T(8,128)(2,1)S(1)} %collective-permute-done.1) | copy-start | bytes 6291460
  65.8 27.3 %collective-permute-start.3 = (bf16[1024,1024]{1,0:T(8,128)(2,1)S(1)}, bf16[1024,1024]{1,0:T(8,128)(2,1)S(1)}, u32[]{:S(2)}, u32[]{:S(2)}) collective-permute-start(bf16[1024,1024]{1,0:T(8,128)(2,1)S(1)} %collective-permute-done.1), channel_id=1, source_target_pairs={{1,0},{2,1},{3,2},{4,3},{5,4},{6,5},{7,6},{8,7},{9,8},{10,9},{11,1... | collective-permute-start | bytes 6291464 | tf_op jit(solution)/shard_map/ppermute | solution.py:15
  93.1 27.5 %copy-start.5 = (bf16[1024,1024]{1,0:T(8,128)(2,1)}, bf16[1024,1024]{1,0:T(8,128)(2,1)S(1)}, u32[]{:S(2)}) copy-start(bf16[1024,1024]{1,0:T(8,128)(2,1)S(1)} %collective-permute-done.3) | copy-start | bytes 6291460
  93.2 27.5 %collective-permute-start.5 = (bf16[1024,1024]{1,0:T(8,128)(2,1)S(1)}, bf16[1024,1024]{1,0:T(8,128)(2,1)}, u32[]{:S(2)}, u32[]{:S(2)}) collective-permute-start(bf16[1024,1024]{1,0:T(8,128)(2,1)S(1)} %collective-permute-done.3), channel_id=1, source_target_pairs={{1,0},{2,1},{3,2},{4,3},{5,4},{6,5},{7,6},{8,7},{9,8},{10,9},{11,1... | collective-permute-start | bytes 6291464 | tf_op jit(solution)/shard_map/ppermute | solution.py:15
  120.6 76.0 %collective-permute-start.7 = (bf16[1024,1024]{1,0:T(8,128)(2,1)}, bf16[1024,1024]{1,0:T(8,128)(2,1)}, u32[]{:S(2)}, u32[]{:S(2)}) collective-permute-start(bf16[1024,1024]{1,0:T(8,128)(2,1)} %collective-permute-done.5), channel_id=1, source_target_pairs={{1,0},{2,1},{3,2},{4,3},{5,4},{6,5},{7,6},{8,7},{9,8},{10,9},{11,1... | collective-permute-start | bytes 6291464 | tf_op jit(solution)/shard_map/ppermute | solution.py:15
  123.1 51.4 %all-to-all-start = ((bf16[16,1,64]{2,1,0:T(2,128)(2,1)}), bf16[16,1,64]{2,1,0:T(2,128)(2,1)S(1)}, u32[]{:S(2)}, u32[]{:S(2)}) async-start(bf16[16,1,64]{2,1,0:T(2,128)(2,1)} %all_to_all.20), calls=%async_computation | async-start | bytes 16384 | tf_op jit(solution)/shard_map/all_to_all | solution.py:53
  174.6 3.0 %collective-permute-start = (bf16[1024]{0:T(1024)(128)(2,1)S(1)}, bf16[1024]{0:T(1024)(128)(2,1)S(1)}, u32[]{:S(2)}, u32[]{:S(2)}) collective-permute-start(bf16[1024]{0:T(1024)(128)(2,1)S(1)} %reshape.97), channel_id=1, source_target_pairs={{1,0},{2,1},{3,2},{4,3},{5,4},{6,5},{7,6},{8,7},{9,8},{10,9},{11,1... | collective-permute-start | bytes 6152 | tf_op jit(solution)/shard_map/ppermute | solution.py:15
  177.7 4.2 %collective-permute-start.2 = (bf16[1024]{0:T(1024)(128)(2,1)S(1)}, bf16[1024]{0:T(1024)(128)(2,1)S(1)}, u32[]{:S(2)}, u32[]{:S(2)}) collective-permute-start(bf16[1024]{0:T(1024)(128)(2,1)S(1)} %collective-permute-done), channel_id=1, source_target_pairs={{1,0},{2,1},{3,2},{4,3},{5,4},{6,5},{7,6},{8,7},{9,8},{10,9},{11,1... | collective-permute-start | bytes 6152 | tf_op jit(solution)/shard_map/ppermute | solution.py:15
  181.9 4.9 %collective-permute-start.4 = (bf16[1024]{0:T(1024)(128)(2,1)S(1)}, bf16[1024]{0:T(1024)(128)(2,1)S(1)}, u32[]{:S(2)}, u32[]{:S(2)}) collective-permute-start(bf16[1024]{0:T(1024)(128)(2,1)S(1)} %collective-permute-done.2), channel_id=1, source_target_pairs={{1,0},{2,1},{3,2},{4,3},{5,4},{6,5},{7,6},{8,7},{9,8},{10,9},{11,1... | collective-permute-start | bytes 6152 | tf_op jit(solution)/shard_map/ppermute | solution.py:15
  186.8 4.9 %collective-permute-start.6 = (bf16[1024]{0:T(1024)(128)(2,1)S(1)}, bf16[1024]{0:T(1024)(128)(2,1)S(1)}, u32[]{:S(2)}, u32[]{:S(2)}) collective-permute-start(bf16[1024]{0:T(1024)(128)(2,1)S(1)} %collective-permute-done.4), channel_id=1, source_target_pairs={{1,0},{2,1},{3,2},{4,3},{5,4},{6,5},{7,6},{8,7},{9,8},{10,9},{11,1... | collective-permute-start | bytes 6152 | tf_op jit(solution)/shard_map/ppermute | solution.py:15
  191.7 4.9 %collective-permute-start.8 = (bf16[1024]{0:T(1024)(128)(2,1)S(1)}, bf16[1024]{0:T(1024)(128)(2,1)S(1)}, u32[]{:S(2)}, u32[]{:S(2)}) collective-permute-start(bf16[1024]{0:T(1024)(128)(2,1)S(1)} %collective-permute-done.6), channel_id=1, source_target_pairs={{1,0},{2,1},{3,2},{4,3},{5,4},{6,5},{7,6},{8,7},{9,8},{10,9},{11,1... | collective-permute-start | bytes 6152 | tf_op jit(solution)/shard_map/ppermute | solution.py:15
  196.6 5.6 %copy-start.6 = (bf16[1024,1024]{1,0:T(8,128)(2,1)S(1)}, bf16[1024,1024]{1,0:T(8,128)(2,1)}, u32[]{:S(2)}) copy-start(bf16[1024,1024]{1,0:T(8,128)(2,1)} %copy-done.5) | copy-start | bytes 6291460
  196.6 16.0 %collective-permute-start.9 = (bf16[1024,1024]{1,0:T(8,128)(2,1)}, bf16[1024,1024]{1,0:T(8,128)(2,1)S(1)}, u32[]{:S(2)}, u32[]{:S(2)}) collective-permute-start(bf16[1024,1024]{1,0:T(8,128)(2,1)} %collective-permute-done.7), channel_id=1, source_target_pairs={{1,0},{2,1},{3,2},{4,3},{5,4},{6,5},{7,6},{8,7},{9,8},{10,9},{11,1... | collective-permute-start | bytes 6291464 | tf_op jit(solution)/shard_map/ppermute | solution.py:15
  212.6 41.2 %copy-start.1 = (s32[512,1]{0,1:T(1,128)S(1)}, s32[512,1]{0,1:T(1,128)}, u32[]{:S(2)}) copy-start(s32[512,1]{0,1:T(1,128)} %param.6) | copy-start | bytes 6148
  220.6 17.8 %collective-permute-start.10 = (f32[1024]{0:T(1024)S(1)}, f32[1024]{0:T(1024)S(1)}, u32[]{:S(2)}, u32[]{:S(2)}) collective-permute-start(f32[1024]{0:T(1024)S(1)} %broadcast_select_fusion), channel_id=1, source_target_pairs={{0,1},{1,2},{2,3},{3,4},{4,5},{5,6},{6,7},{7,8},{8,9},{9,10},{10,1... | collective-permute-start | bytes 12296 | tf_op jit(solution)/shard_map/ppermute | solution.py:15
  238.5 3.0 %collective-permute-start.11 = (f32[1024]{0:T(1024)S(1)}, f32[1024]{0:T(1024)S(1)}, u32[]{:S(2)}, u32[]{:S(2)}) collective-permute-start(f32[1024]{0:T(1024)S(1)} %select_maximum_fusion.3), channel_id=1, source_target_pairs={{0,1},{1,2},{2,3},{3,4},{4,5},{5,6},{6,7},{7,8},{8,9},{9,10},{10,1... | collective-permute-start | bytes 12296 | tf_op jit(solution)/shard_map/ppermute | solution.py:15
  241.5 8.2 %collective-permute-start.12 = (f32[1024]{0:T(1024)S(1)}, f32[1024]{0:T(1024)S(1)}, u32[]{:S(2)}, u32[]{:S(2)}) collective-permute-start(f32[1024]{0:T(1024)S(1)} %select_maximum_fusion.2), channel_id=1, source_target_pairs={{0,1},{1,2},{2,3},{3,4},{4,5},{5,6},{6,7},{7,8},{8,9},{9,10},{10,1... | collective-permute-start | bytes 12296 | tf_op jit(solution)/shard_map/ppermute | solution.py:15
  249.7 4.9 %collective-permute-start.13 = (f32[1024]{0:T(1024)S(1)}, f32[1024]{0:T(1024)S(1)}, u32[]{:S(2)}, u32[]{:S(2)}) collective-permute-start(f32[1024]{0:T(1024)S(1)} %select_maximum_fusion.1), channel_id=1, source_target_pairs={{0,1},{1,2},{2,3},{3,4},{4,5},{5,6},{6,7},{7,8},{8,9},{9,10},{10,1... | collective-permute-start | bytes 12296 | tf_op jit(solution)/shard_map/ppermute | solution.py:15
  254.6 6.6 %collective-permute-start.14 = (f32[1024]{0:T(1024)S(1)}, f32[1024]{0:T(1024)S(1)}, u32[]{:S(2)}, u32[]{:S(2)}) collective-permute-start(f32[1024]{0:T(1024)S(1)} %select_maximum_fusion), channel_id=1, source_target_pairs={{0,1},{1,2},{2,3},{3,4},{4,5},{5,6},{6,7},{7,8},{8,9},{9,10},{10,1... | collective-permute-start | bytes 12296 | tf_op jit(solution)/shard_map/ppermute | solution.py:15
  261.9 15.7 %all-to-all-start.2 = ((f32[16,1,64]{2,1,0:T(1,128)}), f32[16,1,64]{2,1,0:T(1,128)S(1)}, u32[]{:S(2)}, u32[]{:S(2)}) async-start(f32[16,1,64]{2,1,0:T(1,128)} %all_to_all.18), calls=%async_computation.2 | async-start | bytes 16384 | tf_op jit(solution)/shard_map/all_to_all | solution.py:81
where the time goes:
time: 283 us; the launch traced here: 282 us
  waiting for transfers between devices  101 us (36%)
  starting transfers between devices  86.9 us (31%)
  blocking collectives  54.4 us (19%)
  matrix products  26.5 us (9%)
  local copies, waits for them, and re-layouts  5.21 us (2%)
  other arithmetic  4.84 us (2%)
  between operations  3.48 us (1%)
    ppermute x15, waiting for transfers between devices, passed_along(): lax.ppermute(value, axis, [(source, source + steps) for source in range(i...  73.7 us
    all_to_all x1, blocking collectives, per_device(): lax.all_to_all(packed.reshape(owners, capacity, width), 'shard', split_ax...  54.4 us
    ppermute x15, starting transfers between devices, passed_along(): lax.ppermute(value, axis, [(source, source + steps) for source in range(i...  48 us
    all_to_all x1, starting transfers between devices, per_device(): lax.all_to_all(packed_scale.reshape(owners, capacity), 'shard', split_axi...  29.6 us
    dot_general x6, matrix products, scaled_tile(): lax.dot_general(left, right, (((1,), (1,)), ((), ())), preferred_element_...  24.8 us
    all_to_all x1, waiting for transfers between devices, per_device(): lax.all_to_all(packed_scale.reshape(owners, capacity), 'shard', split_axi...  20.4 us
    all_to_all x1, starting transfers between devices, per_device(): lax.all_to_all(slot_best.reshape(owners, capacity), 'shard', split_axis=0...  9.27 us
    all_to_all x1, waiting for transfers between devices, per_device(): lax.all_to_all(slot_best.reshape(owners, capacity), 'shard', split_axis=0...  6.42 us
  transfers between devices with their start and end apart: 17, of which 14 were waited for; matrix products, arithmetic and copies ran while one was open for 6% of the time, Pallas kernels for 0%

commit v1 on v0

--- a/solution.py
+++ b/solution.py
@@ -1,6 +1,10 @@
+import functools
+
 import jax
 import jax.numpy as jnp
 from jax import lax
+from jax.experimental import pallas as pl
+from jax.experimental.pallas import tpu as pltpu
 from jax.sharding import PartitionSpec as P
 
 PARTNERS = 5
@@ -83,6 +87,274 @@
     )
     return jnp.take(homeward.reshape(slots), position)
 
+REACH = 2
+CORES = 2
+LANES = 128
+SUBLANES = 8
+CHUNKS = 4
+OUT = -(2.0**100)
+MESH = pl.DeviceIdType.MESH
+
+OWN, SIB, NEXT, PREV, PREV_SIB, NEXT2, PREV2 = range(7)
+LEFT = {OWN: 0, NEXT: 1, NEXT2: 2}
+TO_SIB, TO_NEXT, TO_PREV, TO_PREV_SIB, TO_NEXT2, TO_PREV2 = range(6)
+
+
+def place(position, core, chips):
+    side = position // (chips // 2)
+    depth = position * (1 - side) + (chips - 1 - position) * side
+    return (depth * 2 + side) * CORES + core
+
+
+def folded(scores):
+    return jnp.max(scores.reshape(scores.shape[0] // SUBLANES, SUBLANES, scores.shape[1]), axis=0)
+
+
+def pair_kernel(
+    owners, x_ref, info_ref, listed_ref, out_ref, emb, info, table, column, barred, across, leave, land,
+    own_best, table_sems, emb_sems, info_sems, home_sems, local_sem,
+):
+    rows, width = x_ref.shape
+    chunk = rows // CHUNKS
+    chips = owners // CORES
+    group = lax.axis_index("groups")
+    me = lax.axis_index("shard")
+    core = lax.rem(me, CORES)
+    chip = me // CORES
+    side = lax.rem(chip, 2)
+    depth = chip // 2
+    position = depth * (1 - side) + (chips - 1 - depth) * side
+
+    def at(step):
+        return lax.rem(position + step + chips, chips)
+
+    def flipped(where):
+        half = where // (chips // 2)
+        return core + half - 2 * core * half
+
+    sibling = place(position, 1 - core, chips)
+    following = place(at(1), core, chips)
+    preceding = place(at(-1), core, chips)
+    crossed = place(at(-1), flipped(at(-1)), chips)
+
+    own_copy = pltpu.make_async_copy(x_ref, emb.at[OWN], local_sem.at[0])
+    own_copy.start()
+    own_listed = pltpu.make_async_copy(listed_ref, table.at[me], local_sem.at[1])
+    own_listed.start()
+
+    barrier = pltpu.get_barrier_semaphore()
+    for other in range(1, owners):
+        pl.semaphore_signal(
+            barrier, inc=1, device_id=(group, lax.rem(me + other, owners)), device_id_type=MESH
+        )
+    pl.semaphore_wait(barrier, owners - 1)
+
+    started = []
+
+    def send(source, target, sems, index, device):
+        copy = pltpu.make_async_remote_copy(
+            src_ref=source,
+            dst_ref=target,
+            send_sem=sems.at[(0, *index)],
+            recv_sem=sems.at[(1, *index)],
+            device_id=(group, device),
+            device_id_type=MESH,
+        )
+        copy.start()
+        started.append(copy)
+        return copy
+
+    def part(slot, k):
+        return emb.at[slot, pl.ds(k * chunk, chunk), :]
+
+    listed = [
+        send(listed_ref, table.at[me], table_sems, (other - 1,), lax.rem(me + other, owners))
+        for other in range(1, owners)
+    ]
+    infos = {
+        SIB: send(info_ref, info.at[SIB], info_sems, (SIB,), sibling),
+        PREV: send(info_ref, info.at[PREV], info_sems, (PREV,), following),
+        NEXT: send(info_ref, info.at[NEXT], info_sems, (NEXT,), preceding),
+    }
+    parts = {}
+    for k in range(CHUNKS):
+        mine = x_ref.at[pl.ds(k * chunk, chunk), :]
+        parts[PREV, k] = send(mine, part(PREV, k), emb_sems, (PREV, k), following)
+        parts[NEXT, k] = send(mine, part(NEXT, k), emb_sems, (NEXT, k), preceding)
+        parts[SIB, k] = send(mine, part(SIB, k), emb_sems, (SIB, k), sibling)
+
+    across[...] = jnp.full(across.shape, OUT, jnp.float32)
+    leave[...] = jnp.full(leave.shape, OUT, jnp.float32)
+    own_best[...] = jnp.full(own_best.shape, OUT, jnp.float32)
+
+    for copy in listed:
+        copy.wait_recv()
+    own_listed.wait()
+    upper = table[:, 0, :owners].astype(jnp.bfloat16)
+
+    def info_of(slot):
+        return info_ref if slot == OWN else info.at[slot]
+
+    def as_left(slot):
+        wide = info_of(slot)[...].astype(jnp.float32)
+        wide = jnp.concatenate([wide, jnp.zeros((LANES - wide.shape[0], rows), jnp.float32)], axis=0)
+        column[LEFT[slot]] = wide.T
+
+    def as_right(slot):
+        named = info_of(slot)[0:owners, :]
+        linked = jnp.dot(upper, named, preferred_element_type=jnp.float32) + lax.dot_general(
+            upper, named, (((0,), (0,)), ((), ())), preferred_element_type=jnp.float32
+        )
+        barred[slot] = jnp.where(linked > 0.5, 0.0, OUT).astype(jnp.bfloat16)
+
+    def meet(left, k, right, first, last, to_right=None, diagonal=False, count=1):
+        span = pl.ds(k * chunk, count * chunk)
+        cols = pl.ds(first * chunk, (last - first) * chunk)
+        about = column[LEFT[left], span, :]
+        scores = lax.dot_general(
+            emb[left, span, :], emb[right, cols, :], (((1,), (1,)), ((), ())),
+            preferred_element_type=jnp.float32,
+        )
+        scores = scores + jnp.dot(
+            about[:, :owners].astype(jnp.bfloat16), barred[right, :, cols],
+            preferred_element_type=jnp.float32,
+        )
+        if diagonal:
+            own_row = lax.broadcasted_iota(jnp.int32, scores.shape, 0) + k * chunk
+            own_col = lax.broadcasted_iota(jnp.int32, scores.shape, 1) + first * chunk
+            scores = jnp.where(own_row == own_col, OUT, scores)
+        scale = info_of(right)[pl.ds(owners, 1), cols].astype(jnp.float32)
+        by_row = scores * scale
+        best = across[LEFT[left], span, :]
+        for lane in range(0, scores.shape[1], LANES):
+            best = jnp.maximum(best, by_row[:, lane : lane + LANES])
+        across[LEFT[left], span, :] = best
+        if to_right is not None:
+            by_col = folded(scores * about[:, owners : owners + 1])
+            to_right[:, cols] = jnp.maximum(to_right[:, cols], by_col)
+
+    def finish_left(left, target):
+        for lane in range(0, rows, LANES):
+            turned = across[LEFT[left], pl.ds(lane, LANES), :].T
+            span = pl.ds(lane, LANES)
+            target[:, span] = jnp.maximum(target[:, span], folded(turned))
+
+    homes = {}
+
+    def send_home(which, device):
+        homes[which] = send(leave.at[which], land.at[which], home_sems, (which,), device)
+
+    as_left(OWN)
+    as_right(OWN)
+    own_copy.wait()
+    for k in range(CHUNKS):
+        meet(OWN, k, OWN, 0, CHUNKS, diagonal=True)
+    infos[SIB].wait_recv()
+    as_right(SIB)
+    for k in range(CHUNKS):
+        parts[SIB, k].wait_recv()
+    for k in range(CHUNKS):
+        meet(OWN, k, SIB, 0, CHUNKS)
+    finish_left(OWN, own_best)
+
+    infos[PREV].wait_recv()
+    infos[NEXT].wait_recv()
+    infos[PREV2] = send(info.at[PREV], info.at[PREV2], info_sems, (PREV2,), following)
+    infos[NEXT2] = send(info.at[NEXT], info.at[NEXT2], info_sems, (NEXT2,), crossed)
+    infos[PREV_SIB] = send(info.at[PREV], info.at[PREV_SIB], info_sems, (PREV_SIB,), sibling)
+    as_left(NEXT)
+    as_right(PREV)
+    for k in range(CHUNKS):
+        parts[PREV, k].wait_recv()
+        parts[PREV2, k] = send(part(PREV, k), part(PREV2, k), emb_sems, (PREV2, k), following)
+        parts[PREV_SIB, k] = send(part(PREV, k), part(PREV_SIB, k), emb_sems, (PREV_SIB, k), sibling)
+        parts[NEXT, k].wait_recv()
+        parts[NEXT2, k] = send(part(NEXT, k), part(NEXT2, k), emb_sems, (NEXT2, k), crossed)
+        meet(NEXT, k, OWN, 0, CHUNKS, own_best)
+        meet(NEXT, k, SIB, 0, CHUNKS, leave.at[TO_SIB])
+    send_home(TO_SIB, sibling)
+    infos[PREV_SIB].wait_recv()
+    as_right(PREV_SIB)
+    for k in range(CHUNKS):
+        parts[PREV_SIB, k].wait_recv()
+    for k in range(CHUNKS):
+        meet(NEXT, k, PREV, 0, CHUNKS, leave.at[TO_PREV])
+        meet(NEXT, k, PREV_SIB, 0, CHUNKS, leave.at[TO_PREV_SIB])
+    finish_left(NEXT, leave.at[TO_NEXT])
+    send_home(TO_NEXT, following)
+
+    infos[PREV2].wait_recv()
+    infos[NEXT2].wait_recv()
+    as_left(NEXT2)
+    as_right(PREV2)
+    for k in range(CHUNKS):
+        parts[NEXT2, k].wait_recv()
+        meet(NEXT2, k, PREV, 0, CHUNKS, leave.at[TO_PREV])
+        meet(NEXT2, k, PREV_SIB, 0, CHUNKS, leave.at[TO_PREV_SIB])
+        if k == CHUNKS - 1:
+            send_home(TO_PREV, preceding)
+            send_home(TO_PREV_SIB, place(at(-1), 1 - core, chips))
+        parts[PREV2, k].wait_recv()
+        meet(NEXT2, k, PREV2, 0, k + 1, leave.at[TO_PREV2])
+        if k:
+            meet(NEXT2, 0, PREV2, k, k + 1, leave.at[TO_PREV2], count=k)
+    send_home(TO_PREV2, place(at(-2), core, chips))
+    finish_left(NEXT2, leave.at[TO_NEXT2])
+    send_home(TO_NEXT2, place(at(2), flipped(position), chips))
+
+    best = own_best[...]
+    for which in homes:
+        homes[which].wait_recv()
+        best = jnp.maximum(best, land[which])
+    scale = info_ref[pl.ds(owners, 1), :].astype(jnp.float32)
+    out_ref[...] = jnp.max(best, axis=0, keepdims=True) * scale
+    for copy in started:
+        copy.wait_send()
+
+
+def all_pairs(embeddings, scales, cluster, pair_listed):
+    rows, width = embeddings.shape
+    owners = lax.axis_size("shard")
+    here = lax.axis_index("shard")
+    names = jnp.arange(owners, dtype=jnp.int32)
+    depth = -(-(owners + 1) // 16) * 16
+    onehot = (names[:, None] == cluster[:, 0][None, :]).astype(jnp.bfloat16)
+    info = jnp.concatenate(
+        [onehot, scales[None, :], jnp.zeros((depth - owners - 1, rows), jnp.bfloat16)], axis=0
+    )
+    lanes = jnp.arange(LANES, dtype=jnp.int32)
+    ahead = lanes[:, None] == here + 1 + jnp.arange(pair_listed.shape[1], dtype=jnp.int32)[None, :]
+    linked = jnp.any(ahead & (pair_listed == 1), axis=1) | (lanes == here)
+    listed = jnp.broadcast_to(linked.astype(jnp.float32)[None, :], (SUBLANES, LANES))
+    vmem = pl.BlockSpec(memory_space=pltpu.VMEM)
+    best = pl.pallas_call(
+        functools.partial(pair_kernel, owners),
+        out_shape=jax.ShapeDtypeStruct((1, rows), jnp.float32),
+        in_specs=[pl.BlockSpec(memory_space=pl.ANY), vmem, vmem],
+        out_specs=vmem,
+        scratch_shapes=[
+            pltpu.VMEM((7, rows, width), jnp.bfloat16),
+            pltpu.VMEM((7, depth, rows), jnp.bfloat16),
+            pltpu.VMEM((owners, SUBLANES, LANES), jnp.float32),
+            pltpu.VMEM((3, rows, LANES), jnp.float32),
+            pltpu.VMEM((7, owners, rows), jnp.bfloat16),
+            pltpu.VMEM((3, rows, LANES), jnp.float32),
+            pltpu.VMEM((6, SUBLANES, rows), jnp.float32),
+            pltpu.VMEM((6, SUBLANES, rows), jnp.float32),
+            pltpu.VMEM((SUBLANES, rows), jnp.float32),
+            pltpu.SemaphoreType.DMA((2, owners - 1)),
+            pltpu.SemaphoreType.DMA((2, 7, CHUNKS)),
+            pltpu.SemaphoreType.DMA((2, 7)),
+            pltpu.SemaphoreType.DMA((2, 6)),
+            pltpu.SemaphoreType.DMA((2,)),
+        ],
+        compiler_params=pltpu.CompilerParams(
+            collective_id=0, has_side_effects=True, vmem_limit_bytes=48 * 2**20
+        ),
+        name="all_pairs",
+    )(embeddings, info, listed)
+    return best.reshape(rows)
+
 
 def solution(mesh):
     placed = (
@@ -91,6 +363,8 @@
         P(("groups", "shard"), None),
         P(("groups", "shard"), None),
     )
+    owners = mesh.shape["shard"]
+    work = all_pairs if owners == 4 * REACH * CORES else per_device
     return jax.shard_map(
-        per_device, mesh=mesh, in_specs=placed, out_specs=P(("groups", "shard")), check_vma=False
-    )
+        work, mesh=mesh, in_specs=placed, out_specs=P(("groups", "shard")), check_vma=False
+    )

time: 283 us -> 64.4 us (0.23)
  waiting for transfers between devices: 101 us -> 0 us
  starting transfers between devices: 86.9 us -> 0 us
  Pallas kernels: 0 us -> 60.7 us
  blocking collectives: 54.4 us -> 0 us
  matrix products: 26.5 us -> 0 us
  other arithmetic: 4.84 us -> 0.19 us
  between operations: 3.48 us -> 0.03 us
    ppermute x15 -> x0, waiting for transfers between devices: 73.7 us -> none  [passed_along(): lax.ppermute(value, axis, [(source, source + steps) for source in range(i...]
    pallas_call x0 -> x1, Pallas kernels: none -> 60.7 us  [all_pairs(): pl.pallas_call(functools.partial(pair_kernel, owners), out_shape=jax.Shap...]
    all_to_all x1 -> x0, blocking collectives: 54.4 us -> none  [per_device(): lax.all_to_all(packed.reshape(owners, capacity, width), 'shard', split_ax...]
    ppermute x15 -> x0, starting transfers between devices: 48 us -> none  [passed_along(): lax.ppermute(value, axis, [(source, source + steps) for source in range(i...]
    all_to_all x2 -> x0, starting transfers between devices: 38.9 us -> none  [the longest x1 29.6 us: per_device(): lax.all_to_all(packed_scale.reshape(owners, capacity), 'shard', split_axi...]
    all_to_all x2 -> x0, waiting for transfers between devices: 26.9 us -> none  [the longest x1 20.4 us: per_device(): lax.all_to_all(packed_scale.reshape(owners, capacity), 'shard', split_axi...]
    dot_general x8 -> x0, matrix products: 26.5 us -> none  [the longest x6 24.8 us: scaled_tile(): lax.dot_general(left, right, (((1,), (1,)), ((), ())), preferred_element_...]
  transfers between devices with their start and end apart: 17 -> 0, of which waited for: 14 -> 0; matrix products, arithmetic and copies ran while one was open for 6% -> 0% of each run, Pallas kernels for 0% -> 0%
where the time goes in v1:
time: 64.4 us; the launch traced here: 64.2 us
  Pallas kernels  60.7 us (94%)
  local copies, waits for them, and re-layouts  3.23 us (5%)
    pallas_call x1, Pallas kernels, all_pairs(): pl.pallas_call(functools.partial(pair_kernel, owners), out_shape=jax.Shap...  60.7 us
    unnamed x7, local copies, waits for them, and re-layouts  2.45 us

profile of v1, /device:TPU:0, one launch (start us, length us, event | category | flops | bytes accessed | tf_op | source)
XLA Modules:
  0.0 64.2 jit_solution(3793803662680375433)
XLA Ops:
  0.0 0.0 copy-start.1
  0.0 0.7 %broadcast_in_dim.6 = bf16[1,512]{1,0:T(2,128)(2,1)S(1)} reshape(bf16[512]{0:T(512)(128)(2,1)} %param.5) | data formatting | bytes 2048 | tf_op jit(solution)/shard_map/broadcast_in_dim | solution.py:323
  0.7 0.0 copy-done.1
  0.7 0.1 pad.2.clone
  0.8 0.1 maximum_maximum_fusion.info_ref
  0.9 0.0 copy-start.2
  0.9 0.6 %copy-done.2 = s32[1,5]{1,0:T(1,128)S(1)} copy-done((s32[1,5]{1,0:T(1,128)S(1)}, s32[1,5]{1,0:T(1,128)}, u32[]{:S(2)}) %copy-start.2) | copy-done | bytes 44
  1.5 0.1 fusion.2
  1.6 0.0 copy-start
  1.7 1.2 %copy-done = bf16[512,1024]{1,0:T(8,128)(2,1)S(1)} copy-done((bf16[512,1024]{1,0:T(8,128)(2,1)S(1)}, bf16[512,1024]{1,0:T(8,128)(2,1)}, u32[]{:S(2)}) %copy-start) | copy-done | bytes 1048600
  2.9 60.7 %all_pairs.1 = f32[1,512]{1,0:T(1,128)S(1)} custom-call(bf16[512,1024]{1,0:T(8,128)(2,1)S(1)} %copy-done, bf16[32,512]{1,0:T(8,128)(2,1)S(1)} %maximum_maximum_fusion.info_ref, f32[8,128]{1,0:T(8,128)S(1)} %broadcast_in_dim.8.listed_ref), custom_call_target="tpu_custom_call" | custom-call | tf_op jit(solution)/shard_map/all_pairs/pallas_call | solution.py:330
  63.6 0.6 copy.6
  (6 shorter events, 0.0 us)
Async XLA Ops:
  0.0 0.7 %copy-start.1 = (s32[512,1]{0,1:T(1,128)S(1)}, s32[512,1]{0,1:T(1,128)}, u32[]{:S(2)}) copy-start(s32[512,1]{0,1:T(1,128)} %param.6) | copy-start | bytes 6148
  0.9 0.7 %copy-start.2 = (s32[1,5]{1,0:T(1,128)S(1)}, s32[1,5]{1,0:T(1,128)}, u32[]{:S(2)}) copy-start(s32[1,5]{1,0:T(1,128)} %param.7) | copy-start | bytes 64
  1.6 1.2 %copy-start = (bf16[512,1024]{1,0:T(8,128)(2,1)S(1)}, bf16[512,1024]{1,0:T(8,128)(2,1)}, u32[]{:S(2)}) copy-start(bf16[512,1024]{1,0:T(8,128)(2,1)} %x_ref.1) | copy-start | bytes 3145732

commit v2 on v1

--- a/solution.py
+++ b/solution.py
@@ -167,14 +167,20 @@
     def part(slot, k):
         return emb.at[slot, pl.ds(k * chunk, chunk), :]
 
-    listed = [
-        send(listed_ref, table.at[me], table_sems, (other - 1,), lax.rem(me + other, owners))
-        for other in range(1, owners)
-    ]
+    def send_info(slot, device):
+        return send(info_ref, info.at[slot], info_sems, (slot,), device)
+
+    listed = []
+    for other in range(1, owners):
+        target = lax.rem(me + other, owners)
+        listed.append(send(listed_ref, table.at[me], table_sems, (other - 1,), target))
     infos = {
-        SIB: send(info_ref, info.at[SIB], info_sems, (SIB,), sibling),
-        PREV: send(info_ref, info.at[PREV], info_sems, (PREV,), following),
-        NEXT: send(info_ref, info.at[NEXT], info_sems, (NEXT,), preceding),
+        SIB: send_info(SIB, sibling),
+        PREV: send_info(PREV, following),
+        NEXT: send_info(NEXT, preceding),
+        PREV_SIB: send_info(PREV_SIB, place(at(1), 1 - core, chips)),
+        PREV2: send_info(PREV2, place(at(2), core, chips)),
+        NEXT2: send_info(NEXT2, place(at(-2), flipped(at(-2)), chips)),
     }
     parts = {}
     for k in range(CHUNKS):
@@ -195,13 +201,17 @@
     def info_of(slot):
         return info_ref if slot == OWN else info.at[slot]
 
+    def named_of(slot, names):
+        name = lax.broadcasted_iota(jnp.int32, (names, rows), 0).astype(jnp.float32)
+        return (info_of(slot)[:, 0:rows] == name).astype(jnp.float32)
+
     def as_left(slot):
-        wide = info_of(slot)[...].astype(jnp.float32)
-        wide = jnp.concatenate([wide, jnp.zeros((LANES - wide.shape[0], rows), jnp.float32)], axis=0)
+        depth = lax.broadcasted_iota(jnp.int32, (LANES, rows), 0)
+        wide = jnp.where(depth == owners, info_of(slot)[:, rows:], named_of(slot, LANES))
         column[LEFT[slot]] = wide.T
 
     def as_right(slot):
-        named = info_of(slot)[0:owners, :]
+        named = named_of(slot, owners).astype(jnp.bfloat16)
         linked = jnp.dot(upper, named, preferred_element_type=jnp.float32) + lax.dot_general(
             upper, named, (((0,), (0,)), ((), ())), preferred_element_type=jnp.float32
         )
@@ -223,7 +233,7 @@
             own_row = lax.broadcasted_iota(jnp.int32, scores.shape, 0) + k * chunk
             own_col = lax.broadcasted_iota(jnp.int32, scores.shape, 1) + first * chunk
             scores = jnp.where(own_row == own_col, OUT, scores)
-        scale = info_of(right)[pl.ds(owners, 1), cols].astype(jnp.float32)
+        scale = info_of(right)[:, pl.ds(rows + first * chunk, (last - first) * chunk)]
         by_row = scores * scale
         best = across[LEFT[left], span, :]
         for lane in range(0, scores.shape[1], LANES):
@@ -259,9 +269,6 @@
 
     infos[PREV].wait_recv()
     infos[NEXT].wait_recv()
-    infos[PREV2] = send(info.at[PREV], info.at[PREV2], info_sems, (PREV2,), following)
-    infos[NEXT2] = send(info.at[NEXT], info.at[NEXT2], info_sems, (NEXT2,), crossed)
-    infos[PREV_SIB] = send(info.at[PREV], info.at[PREV_SIB], info_sems, (PREV_SIB,), sibling)
     as_left(NEXT)
     as_right(PREV)
     for k in range(CHUNKS):
@@ -306,7 +313,7 @@
     for which in homes:
         homes[which].wait_recv()
         best = jnp.maximum(best, land[which])
-    scale = info_ref[pl.ds(owners, 1), :].astype(jnp.float32)
+    scale = info_ref[:, rows:]
     out_ref[...] = jnp.max(best, axis=0, keepdims=True) * scale
     for copy in started:
         copy.wait_send()
@@ -316,26 +323,24 @@
     rows, width = embeddings.shape
     owners = lax.axis_size("shard")
     here = lax.axis_index("shard")
-    names = jnp.arange(owners, dtype=jnp.int32)
-    depth = -(-(owners + 1) // 16) * 16
-    onehot = (names[:, None] == cluster[:, 0][None, :]).astype(jnp.bfloat16)
     info = jnp.concatenate(
-        [onehot, scales[None, :], jnp.zeros((depth - owners - 1, rows), jnp.bfloat16)], axis=0
+        [cluster.reshape(1, rows).astype(jnp.float32), scales.reshape(1, rows).astype(jnp.float32)],
+        axis=1,
     )
     lanes = jnp.arange(LANES, dtype=jnp.int32)
     ahead = lanes[:, None] == here + 1 + jnp.arange(pair_listed.shape[1], dtype=jnp.int32)[None, :]
     linked = jnp.any(ahead & (pair_listed == 1), axis=1) | (lanes == here)
-    listed = jnp.broadcast_to(linked.astype(jnp.float32)[None, :], (SUBLANES, LANES))
+    listed = linked.astype(jnp.float32)[None, :]
     vmem = pl.BlockSpec(memory_space=pltpu.VMEM)
     best = pl.pallas_call(
         functools.partial(pair_kernel, owners),
         out_shape=jax.ShapeDtypeStruct((1, rows), jnp.float32),
-        in_specs=[pl.BlockSpec(memory_space=pl.ANY), vmem, vmem],
+        in_specs=[pl.BlockSpec(memory_space=pltpu.HBM), vmem, vmem],
         out_specs=vmem,
         scratch_shapes=[
             pltpu.VMEM((7, rows, width), jnp.bfloat16),
-            pltpu.VMEM((7, depth, rows), jnp.bfloat16),
-            pltpu.VMEM((owners, SUBLANES, LANES), jnp.float32),
+            pltpu.VMEM((7, 1, 2 * rows), jnp.float32),
+            pltpu.VMEM((owners, 1, LANES), jnp.float32),
             pltpu.VMEM((3, rows, LANES), jnp.float32),
             pltpu.VMEM((7, owners, rows), jnp.bfloat16),
             pltpu.VMEM((3, rows, LANES), jnp.float32),

time: 64.4 us -> 62.1 us (0.964)
  Pallas kernels: 60.7 us -> 58.6 us
  local copies, waits for them, and re-layouts: 3.23 us -> 2.45 us
    pallas_call x1, Pallas kernels: 60.7 us -> 58.6 us  [all_pairs(): pl.pallas_call(functools.partial(pair_kernel, owners), out_shape=jax.Shap...]
    broadcast_in_dim x3 -> x0, local copies, waits for them, and re-layouts: 0.7 us -> none  [the longest x1 0.7 us: all_pairs(): scales[None, :]]
    convert_element_type x2 -> x3, other arithmetic: 0.02 us -> 0.71 us  [the longest x1 0.69 us: all_pairs(): scales.reshape(1, rows).astype(jnp.float32)]
where the time goes in v2:
time: 62.1 us; the launch traced here: 61.9 us
  Pallas kernels  58.6 us (94%)
  local copies, waits for them, and re-layouts  2.45 us (4%)
  other arithmetic  0.82 us (1%)
    pallas_call x1, Pallas kernels, all_pairs(): pl.pallas_call(functools.partial(pair_kernel, owners), out_shape=jax.Shap...  58.6 us
    unnamed x7, local copies, waits for them, and re-layouts  2.45 us

profile of v2, /device:TPU:0, one launch (start us, length us, event | category | flops | bytes accessed | tf_op | source)
XLA Modules:
  0.0 61.9 jit_solution(987484428093161614)
XLA Ops:
  0.0 0.0 copy-start.1
  0.0 0.7 %convert_element_type.35 = f32[512]{0:T(512)S(1)} convert(bf16[512]{0:T(512)(128)(2,1)} %param.5) | non-fusion elementwise | flops 512 | bytes 3072 | tf_op jit(solution)/shard_map/convert_element_type | solution.py:327
  0.7 0.0 copy-done.1
  0.7 0.0 copy-start.2
  0.7 0.6 %copy-done.2 = s32[1,5]{1,0:T(1,128)S(1)} copy-done((s32[1,5]{1,0:T(1,128)S(1)}, s32[1,5]{1,0:T(1,128)}, u32[]{:S(2)}) %copy-start.2) | copy-done | bytes 44
  1.4 0.1 fusion.1
  1.5 0.0 copy-start
  1.5 1.2 %copy-done = bf16[512,1024]{1,0:T(8,128)(2,1)S(1)} copy-done((bf16[512,1024]{1,0:T(8,128)(2,1)S(1)}, bf16[512,1024]{1,0:T(8,128)(2,1)}, u32[]{:S(2)}) %copy-start) | copy-done | bytes 1048600
  2.7 58.6 %all_pairs.1 = f32[1,512]{1,0:T(1,128)S(1)} custom-call(bf16[512,1024]{1,0:T(8,128)(2,1)S(1)} %copy-done, f32[1,1024]{1,0:T(1,128)S(1)} %pad_maximum_fusion.info_ref, f32[1,128]{1,0:T(1,128)S(1)} %fusion.2.listed_ref), custom_call_target="tpu_custom_call" | custom-call | tf_op jit(solution)/shard_map/all_pairs/pallas_call | solution.py:335
  61.3 0.6 copy.6
  (5 shorter events, 0.0 us)
Async XLA Ops:
  0.0 0.7 %copy-start.1 = (s32[512,1]{0,1:T(1,128)S(1)}, s32[512,1]{0,1:T(1,128)}, u32[]{:S(2)}) copy-start(s32[512,1]{0,1:T(1,128)} %param.6) | copy-start | bytes 6148
  0.7 0.7 %copy-start.2 = (s32[1,5]{1,0:T(1,128)S(1)}, s32[1,5]{1,0:T(1,128)}, u32[]{:S(2)}) copy-start(s32[1,5]{1,0:T(1,128)} %param.7) | copy-start | bytes 64
  1.5 1.2 %copy-start = (bf16[512,1024]{1,0:T(8,128)(2,1)S(1)}, bf16[512,1024]{1,0:T(8,128)(2,1)}, u32[]{:S(2)}) copy-start(bf16[512,1024]{1,0:T(8,128)(2,1)} %x_ref.1) | copy-start | bytes 3145732

commit v3 on v2

--- a/solution.py
+++ b/solution.py
@@ -95,9 +95,12 @@
 OUT = -(2.0**100)
 MESH = pl.DeviceIdType.MESH
 
-OWN, SIB, NEXT, PREV, PREV_SIB, NEXT2, PREV2 = range(7)
-LEFT = {OWN: 0, NEXT: 1, NEXT2: 2}
-TO_SIB, TO_NEXT, TO_PREV, TO_PREV_SIB, TO_NEXT2, TO_PREV2 = range(6)
+OWN, SIB, NEXT, PREV, PREV_SIB, NEXT2, PREV2, NEXT_SIB, PREV2_SIB, RUNG = range(10)
+LEFT = {OWN: 0, NEXT: 1, NEXT2: 2, PREV2: 3, RUNG: 4}
+RELAYED = 1
+(
+    TO_SIB, TO_NEXT, TO_PREV, TO_PREV_SIB, TO_NEXT2, TO_PREV2, TO_NEXT_SIB, TO_PREV2_SIB, TO_RUNG
+) = range(9)
 
 
 def place(position, core, chips):
@@ -112,7 +115,7 @@
 
 def pair_kernel(
     owners, x_ref, info_ref, listed_ref, out_ref, emb, info, table, column, barred, across, leave, land,
-    own_best, table_sems, emb_sems, info_sems, home_sems, local_sem,
+    lent, own_best, lent_sems, table_sems, emb_sems, info_sems, home_sems, local_sem,
 ):
     rows, width = x_ref.shape
     chunk = rows // CHUNKS
@@ -128,14 +131,21 @@
     def at(step):
         return lax.rem(position + step + chips, chips)
 
-    def flipped(where):
-        half = where // (chips // 2)
-        return core + half - 2 * core * half
-
+    def is_full(step, whose):
+        there = at(step)
+        turn = there // (chips // 2)
+        down = there * (1 - turn) + (chips - 1 - there) * turn
+        return lax.rem(down + whose, 2) == 0
+
+    full, full_next, full_prev = is_full(0, group), is_full(1, group), is_full(-1, group)
+    light, light_next, light_prev = is_full(0, group + 1), is_full(1, group + 1), is_full(-1, group + 1)
+    on_rung = jnp.where(depth == chips // 4 - group, 1, 0)
+    rung_from = on_rung + side == 2
+    rung_to = on_rung - side == 1
+    opposite = place(chips - 1 - position, core, chips)
     sibling = place(position, 1 - core, chips)
     following = place(at(1), core, chips)
     preceding = place(at(-1), core, chips)
-    crossed = place(at(-1), flipped(at(-1)), chips)
 
     own_copy = pltpu.make_async_copy(x_ref, emb.at[OWN], local_sem.at[0])
     own_copy.start()
@@ -147,21 +157,26 @@
         pl.semaphore_signal(
             barrier, inc=1, device_id=(group, lax.rem(me + other, owners)), device_id_type=MESH
         )
-    pl.semaphore_wait(barrier, owners - 1)
+    pl.semaphore_signal(barrier, inc=1, device_id=(1 - group, me), device_id_type=MESH)
+    pl.semaphore_wait(barrier, owners)
 
     started = []
 
-    def send(source, target, sems, index, device):
+    def send(source, target, sems, index, device, only=None, whose=group):
         copy = pltpu.make_async_remote_copy(
             src_ref=source,
             dst_ref=target,
             send_sem=sems.at[(0, *index)],
             recv_sem=sems.at[(1, *index)],
-            device_id=(group, device),
+            device_id=(whose, device),
             device_id_type=MESH,
         )
-        copy.start()
-        started.append(copy)
+        if only is None:
+            copy.start()
+        elif only is not False:
+            pl.when(only)(copy.start)
+        if only is not False:
+            started.append((copy, only))
         return copy
 
     def part(slot, k):
@@ -180,7 +195,10 @@
         NEXT: send_info(NEXT, preceding),
         PREV_SIB: send_info(PREV_SIB, place(at(1), 1 - core, chips)),
         PREV2: send_info(PREV2, place(at(2), core, chips)),
-        NEXT2: send_info(NEXT2, place(at(-2), flipped(at(-2)), chips)),
+        NEXT2: send_info(NEXT2, place(at(-2), core, chips)),
+        NEXT_SIB: send_info(NEXT_SIB, place(at(-1), 1 - core, chips)),
+        PREV2_SIB: send_info(PREV2_SIB, place(at(2), 1 - core, chips)),
+        RUNG: send_info(RUNG, opposite),
     }
     parts = {}
     for k in range(CHUNKS):
@@ -188,6 +206,7 @@
         parts[PREV, k] = send(mine, part(PREV, k), emb_sems, (PREV, k), following)
         parts[NEXT, k] = send(mine, part(NEXT, k), emb_sems, (NEXT, k), preceding)
         parts[SIB, k] = send(mine, part(SIB, k), emb_sems, (SIB, k), sibling)
+        parts[RUNG, k] = send(mine, part(RUNG, k), emb_sems, (RUNG, k), opposite, rung_from)
 
     across[...] = jnp.full(across.shape, OUT, jnp.float32)
     leave[...] = jnp.full(leave.shape, OUT, jnp.float32)
@@ -267,47 +286,113 @@
         meet(OWN, k, SIB, 0, CHUNKS)
     finish_left(OWN, own_best)
 
-    infos[PREV].wait_recv()
-    infos[NEXT].wait_recv()
+    for slot in (PREV, NEXT, PREV_SIB, PREV2, NEXT2, NEXT_SIB, PREV2_SIB, RUNG):
+        infos[slot].wait_recv()
     as_left(NEXT)
     as_right(PREV)
+    as_right(PREV_SIB)
+    relays = {}
+
+    def pass_on(slot, far, k, device, wanted):
+        way = 0 if slot == PREV else 1
+        if k < RELAYED:
+            relays[0, way, k] = send(
+                part(slot, k), lent.at[0, way, k], lent_sems, (0, way, k), me, wanted, 1 - group
+            )
+            parts[far, k] = send(
+                lent.at[1, way, k], part(far, k), emb_sems, (far, k), me, False, 1 - group
+            )
+        else:
+            parts[far, k] = send(part(slot, k), part(far, k), emb_sems, (far, k), device, wanted)
+
+    def relay(first, way, k, wanted, device, whose):
+        @pl.when(wanted)
+        def _():
+            relays[first, way, k].wait_recv()
+
+        if first == 0:
+            relays[1, way, k] = send(
+                lent.at[0, way, k], lent.at[1, way, k], lent_sems, (1, way, k), device, wanted
+            )
+
     for k in range(CHUNKS):
         parts[PREV, k].wait_recv()
-        parts[PREV2, k] = send(part(PREV, k), part(PREV2, k), emb_sems, (PREV2, k), following)
+        pass_on(PREV, PREV2, k, following, full_next)
         parts[PREV_SIB, k] = send(part(PREV, k), part(PREV_SIB, k), emb_sems, (PREV_SIB, k), sibling)
         parts[NEXT, k].wait_recv()
-        parts[NEXT2, k] = send(part(NEXT, k), part(NEXT2, k), emb_sems, (NEXT2, k), crossed)
+        pass_on(NEXT, NEXT2, k, preceding, full_prev)
+        parts[NEXT_SIB, k] = send(part(NEXT, k), part(NEXT_SIB, k), emb_sems, (NEXT_SIB, k), sibling)
+        if 0 < k <= RELAYED:
+            relay(0, 0, k - 1, light_next, following, group)
+            relay(0, 1, k - 1, light_prev, preceding, group)
         meet(NEXT, k, OWN, 0, CHUNKS, own_best)
         meet(NEXT, k, SIB, 0, CHUNKS, leave.at[TO_SIB])
-    send_home(TO_SIB, sibling)
-    infos[PREV_SIB].wait_recv()
-    as_right(PREV_SIB)
     for k in range(CHUNKS):
         parts[PREV_SIB, k].wait_recv()
+        parts[NEXT_SIB, k].wait_recv()
     for k in range(CHUNKS):
         meet(NEXT, k, PREV, 0, CHUNKS, leave.at[TO_PREV])
         meet(NEXT, k, PREV_SIB, 0, CHUNKS, leave.at[TO_PREV_SIB])
     finish_left(NEXT, leave.at[TO_NEXT])
+
+    @pl.when(rung_to)
+    def _():
+        as_left(RUNG)
+        for k in range(CHUNKS):
+            parts[RUNG, k].wait_recv()
+            meet(RUNG, k, OWN, 0, CHUNKS, own_best)
+            meet(RUNG, k, SIB, 0, CHUNKS, leave.at[TO_SIB])
+        finish_left(RUNG, leave.at[TO_RUNG])
+
+    send_home(TO_SIB, sibling)
+    send_home(TO_RUNG, opposite)
+
+    for k in range(RELAYED):
+        for way in range(2):
+            relay(1, way, k, light, None, None)
+            far = NEXT2 if way else PREV2
+            pl.when(light)(parts[far, k].start)
+            started.append((parts[far, k], light))
+
+    @pl.when(full)
+    def _():
+        for slot in (NEXT2, PREV2):
+            as_left(slot)
+        for slot in (NEXT, NEXT_SIB, PREV2, PREV2_SIB):
+            as_right(slot)
+        shared = []
+        for k in (*range(RELAYED, CHUNKS), *range(RELAYED)):
+            parts[PREV2, k].wait_recv()
+            copy = pltpu.make_async_remote_copy(
+                src_ref=part(PREV2, k),
+                dst_ref=part(PREV2_SIB, k),
+                send_sem=emb_sems.at[0, PREV2_SIB, k],
+                recv_sem=emb_sems.at[1, PREV2_SIB, k],
+                device_id=(group, sibling),
+                device_id_type=MESH,
+            )
+            copy.start()
+            shared.append(copy)
+            meet(PREV2, k, NEXT, 0, CHUNKS, leave.at[TO_NEXT])
+            meet(PREV2, k, NEXT_SIB, 0, CHUNKS, leave.at[TO_NEXT_SIB])
+            parts[NEXT2, k].wait_recv()
+            meet(NEXT2, k, PREV, 0, CHUNKS, leave.at[TO_PREV])
+            meet(NEXT2, k, PREV_SIB, 0, CHUNKS, leave.at[TO_PREV_SIB])
+        for copy in shared:
+            copy.wait()
+        for k in range(CHUNKS):
+            meet(NEXT2, k, PREV2, 0, CHUNKS, leave.at[TO_PREV2])
+            meet(NEXT2, k, PREV2_SIB, 0, CHUNKS, leave.at[TO_PREV2_SIB])
+        finish_left(NEXT2, leave.at[TO_NEXT2])
+        finish_left(PREV2, leave.at[TO_PREV2])
+
     send_home(TO_NEXT, following)
-
-    infos[PREV2].wait_recv()
-    infos[NEXT2].wait_recv()
-    as_left(NEXT2)
-    as_right(PREV2)
-    for k in range(CHUNKS):
-        parts[NEXT2, k].wait_recv()
-        meet(NEXT2, k, PREV, 0, CHUNKS, leave.at[TO_PREV])
-        meet(NEXT2, k, PREV_SIB, 0, CHUNKS, leave.at[TO_PREV_SIB])
-        if k == CHUNKS - 1:
-            send_home(TO_PREV, preceding)
-            send_home(TO_PREV_SIB, place(at(-1), 1 - core, chips))
-        parts[PREV2, k].wait_recv()
-        meet(NEXT2, k, PREV2, 0, k + 1, leave.at[TO_PREV2])
-        if k:
-            meet(NEXT2, 0, PREV2, k, k + 1, leave.at[TO_PREV2], count=k)
+    send_home(TO_NEXT_SIB, place(at(1), 1 - core, chips))
+    send_home(TO_PREV, preceding)
+    send_home(TO_PREV_SIB, place(at(-1), 1 - core, chips))
+    send_home(TO_NEXT2, place(at(2), core, chips))
     send_home(TO_PREV2, place(at(-2), core, chips))
-    finish_left(NEXT2, leave.at[TO_NEXT2])
-    send_home(TO_NEXT2, place(at(2), flipped(position), chips))
+    send_home(TO_PREV2_SIB, place(at(-2), 1 - core, chips))
 
     best = own_best[...]
     for which in homes:
@@ -315,8 +400,11 @@
         best = jnp.maximum(best, land[which])
     scale = info_ref[:, rows:]
     out_ref[...] = jnp.max(best, axis=0, keepdims=True) * scale
-    for copy in started:
-        copy.wait_send()
+    for copy, only in started:
+        if only is None:
+            copy.wait_send()
+        else:
+            pl.when(only)(copy.wait_send)
 
 
 def all_pairs(embeddings, scales, cluster, pair_listed):
@@ -338,19 +426,21 @@
         in_specs=[pl.BlockSpec(memory_space=pltpu.HBM), vmem, vmem],
         out_specs=vmem,
         scratch_shapes=[
-            pltpu.VMEM((7, rows, width), jnp.bfloat16),
-            pltpu.VMEM((7, 1, 2 * rows), jnp.float32),
+            pltpu.VMEM((10, rows, width), jnp.bfloat16),
+            pltpu.VMEM((10, 1, 2 * rows), jnp.float32),
             pltpu.VMEM((owners, 1, LANES), jnp.float32),
-            pltpu.VMEM((3, rows, LANES), jnp.float32),
-            pltpu.VMEM((7, owners, rows), jnp.bfloat16),
-            pltpu.VMEM((3, rows, LANES), jnp.float32),
-            pltpu.VMEM((6, SUBLANES, rows), jnp.float32),
-            pltpu.VMEM((6, SUBLANES, rows), jnp.float32),
+            pltpu.VMEM((5, rows, LANES), jnp.float32),
+            pltpu.VMEM((10, owners, rows), jnp.bfloat16),
+            pltpu.VMEM((5, rows, LANES), jnp.float32),
+            pltpu.VMEM((9, SUBLANES, rows), jnp.float32),
+            pltpu.VMEM((9, SUBLANES, rows), jnp.float32),
+            pltpu.VMEM((2, 2, RELAYED, rows // CHUNKS, width), jnp.bfloat16),
             pltpu.VMEM((SUBLANES, rows), jnp.float32),
+            pltpu.SemaphoreType.DMA((2, 2, 2, RELAYED)),
             pltpu.SemaphoreType.DMA((2, owners - 1)),
-            pltpu.SemaphoreType.DMA((2, 7, CHUNKS)),
-            pltpu.SemaphoreType.DMA((2, 7)),
-            pltpu.SemaphoreType.DMA((2, 6)),
+            pltpu.SemaphoreType.DMA((2, 10, CHUNKS)),
+            pltpu.SemaphoreType.DMA((2, 10)),
+            pltpu.SemaphoreType.DMA((2, 9)),
             pltpu.SemaphoreType.DMA((2,)),
         ],
         compiler_params=pltpu.CompilerParams(
@@ -369,7 +459,7 @@
         P(("groups", "shard"), None),
     )
     owners = mesh.shape["shard"]
-    work = all_pairs if owners == 4 * REACH * CORES else per_device
+    work = all_pairs if owners == 4 * REACH * CORES and mesh.shape["groups"] == 2 else per_device
     return jax.shard_map(
         work, mesh=mesh, in_specs=placed, out_specs=P(("groups", "shard")), check_vma=False
     )

time: 62.1 us -> 63.7 us (1.026)
  Pallas kernels: 58.6 us -> 60.2 us
    pallas_call x1, Pallas kernels: 58.6 us -> 60.2 us  [all_pairs(): pl.pallas_call(functools.partial(pair_kernel, owners), out_shape=jax.Shap...]
where the time goes in v3:
time: 63.7 us; the launch traced here: 63.5 us
  Pallas kernels  60.2 us (95%)
  local copies, waits for them, and re-layouts  2.45 us (4%)
  other arithmetic  0.82 us (1%)
    pallas_call x1, Pallas kernels, all_pairs(): pl.pallas_call(functools.partial(pair_kernel, owners), out_shape=jax.Shap...  60.2 us
    unnamed x7, local copies, waits for them, and re-layouts  2.45 us

profile of v3, /device:TPU:0, one launch (start us, length us, event | category | flops | bytes accessed | tf_op | source)
XLA Modules:
  0.0 63.5 jit_solution(10135988394506596579)
XLA Ops:
  0.0 0.0 copy-start.1
  0.0 0.7 %convert_element_type.35 = f32[512]{0:T(512)S(1)} convert(bf16[512]{0:T(512)(128)(2,1)} %param.5) | non-fusion elementwise | flops 512 | bytes 3072 | tf_op jit(solution)/shard_map/convert_element_type | solution.py:415
  0.7 0.0 copy-done.1
  0.7 0.0 copy-start.2
  0.7 0.6 %copy-done.2 = s32[1,5]{1,0:T(1,128)S(1)} copy-done((s32[1,5]{1,0:T(1,128)S(1)}, s32[1,5]{1,0:T(1,128)}, u32[]{:S(2)}) %copy-start.2) | copy-done | bytes 44
  1.4 0.1 fusion.1
  1.5 0.0 copy-start
  1.5 1.2 %copy-done = bf16[512,1024]{1,0:T(8,128)(2,1)S(1)} copy-done((bf16[512,1024]{1,0:T(8,128)(2,1)S(1)}, bf16[512,1024]{1,0:T(8,128)(2,1)}, u32[]{:S(2)}) %copy-start) | copy-done | bytes 1048600
  2.7 60.2 %all_pairs.1 = f32[1,512]{1,0:T(1,128)S(1)} custom-call(bf16[512,1024]{1,0:T(8,128)(2,1)S(1)} %copy-done, f32[1,1024]{1,0:T(1,128)S(1)} %pad_maximum_fusion.info_ref, f32[1,128]{1,0:T(1,128)S(1)} %fusion.2.listed_ref), custom_call_target="tpu_custom_call" | custom-call | tf_op jit(solution)/shard_map/all_pairs/pallas_call | solution.py:423
  62.9 0.6 copy.6
  (5 shorter events, 0.0 us)
Async XLA Ops:
  0.0 0.7 %copy-start.1 = (s32[512,1]{0,1:T(1,128)S(1)}, s32[512,1]{0,1:T(1,128)}, u32[]{:S(2)}) copy-start(s32[512,1]{0,1:T(1,128)} %param.6) | copy-start | bytes 6148
  0.7 0.7 %copy-start.2 = (s32[1,5]{1,0:T(1,128)S(1)}, s32[1,5]{1,0:T(1,128)}, u32[]{:S(2)}) copy-start(s32[1,5]{1,0:T(1,128)} %param.7) | copy-start | bytes 64
  1.5 1.2 %copy-start = (bf16[512,1024]{1,0:T(8,128)(2,1)S(1)}, bf16[512,1024]{1,0:T(8,128)(2,1)}, u32[]{:S(2)}) copy-start(bf16[512,1024]{1,0:T(8,128)(2,1)} %x_ref.1) | copy-start | bytes 3145732

commit v4 on v3

--- a/solution.py
+++ b/solution.py
@@ -360,7 +360,7 @@
             as_left(slot)
         for slot in (NEXT, NEXT_SIB, PREV2, PREV2_SIB):
             as_right(slot)
-        shared = []
+        seen = []
         for k in (*range(RELAYED, CHUNKS), *range(RELAYED)):
             parts[PREV2, k].wait_recv()
             copy = pltpu.make_async_remote_copy(
@@ -372,17 +372,19 @@
                 device_id_type=MESH,
             )
             copy.start()
-            shared.append(copy)
             meet(PREV2, k, NEXT, 0, CHUNKS, leave.at[TO_NEXT])
             meet(PREV2, k, NEXT_SIB, 0, CHUNKS, leave.at[TO_NEXT_SIB])
             parts[NEXT2, k].wait_recv()
             meet(NEXT2, k, PREV, 0, CHUNKS, leave.at[TO_PREV])
             meet(NEXT2, k, PREV_SIB, 0, CHUNKS, leave.at[TO_PREV_SIB])
-        for copy in shared:
             copy.wait()
-        for k in range(CHUNKS):
-            meet(NEXT2, k, PREV2, 0, CHUNKS, leave.at[TO_PREV2])
-            meet(NEXT2, k, PREV2_SIB, 0, CHUNKS, leave.at[TO_PREV2_SIB])
+            for j in seen:
+                for right, home in ((PREV2, TO_PREV2), (PREV2_SIB, TO_PREV2_SIB)):
+                    meet(NEXT2, k, right, j, j + 1, leave.at[home])
+                    meet(NEXT2, j, right, k, k + 1, leave.at[home])
+            for right, home in ((PREV2, TO_PREV2), (PREV2_SIB, TO_PREV2_SIB)):
+                meet(NEXT2, k, right, k, k + 1, leave.at[home])
+            seen.append(k)
         finish_left(NEXT2, leave.at[TO_NEXT2])
         finish_left(PREV2, leave.at[TO_PREV2])
 

time: 63.7 us -> 63.1 us (level)
  no operation moved by 1% of the time
where the time goes in v4:
time: 63.1 us; the launch traced here: 62.9 us
  Pallas kernels  59.6 us (94%)
  local copies, waits for them, and re-layouts  2.45 us (4%)
  other arithmetic  0.82 us (1%)
    pallas_call x1, Pallas kernels, all_pairs(): pl.pallas_call(functools.partial(pair_kernel, owners), out_shape=jax.Shap...  59.6 us
    unnamed x7, local copies, waits for them, and re-layouts  2.45 us

profile of v4, /device:TPU:0, one launch (start us, length us, event | category | flops | bytes accessed | tf_op | source)
XLA Modules:
  0.0 62.9 jit_solution(680577060612765859)
XLA Ops:
  0.0 0.0 copy-start.1
  0.0 0.7 %convert_element_type.35 = f32[512]{0:T(512)S(1)} convert(bf16[512]{0:T(512)(128)(2,1)} %param.5) | non-fusion elementwise | flops 512 | bytes 3072 | tf_op jit(solution)/shard_map/convert_element_type | solution.py:417
  0.7 0.0 copy-done.1
  0.7 0.0 copy-start.2
  0.7 0.6 %copy-done.2 = s32[1,5]{1,0:T(1,128)S(1)} copy-done((s32[1,5]{1,0:T(1,128)S(1)}, s32[1,5]{1,0:T(1,128)}, u32[]{:S(2)}) %copy-start.2) | copy-done | bytes 44
  1.4 0.1 fusion.1
  1.5 0.0 copy-start
  1.5 1.2 %copy-done = bf16[512,1024]{1,0:T(8,128)(2,1)S(1)} copy-done((bf16[512,1024]{1,0:T(8,128)(2,1)S(1)}, bf16[512,1024]{1,0:T(8,128)(2,1)}, u32[]{:S(2)}) %copy-start) | copy-done | bytes 1048600
  2.7 59.6 %all_pairs.1 = f32[1,512]{1,0:T(1,128)S(1)} custom-call(bf16[512,1024]{1,0:T(8,128)(2,1)S(1)} %copy-done, f32[1,1024]{1,0:T(1,128)S(1)} %pad_maximum_fusion.info_ref, f32[1,128]{1,0:T(1,128)S(1)} %fusion.2.listed_ref), custom_call_target="tpu_custom_call" | custom-call | tf_op jit(solution)/shard_map/all_pairs/pallas_call | solution.py:425
  62.3 0.6 copy.6
  (5 shorter events, 0.0 us)
Async XLA Ops:
  0.0 0.7 %copy-start.1 = (s32[512,1]{0,1:T(1,128)S(1)}, s32[512,1]{0,1:T(1,128)}, u32[]{:S(2)}) copy-start(s32[512,1]{0,1:T(1,128)} %param.6) | copy-start | bytes 6148
  0.7 0.7 %copy-start.2 = (s32[1,5]{1,0:T(1,128)S(1)}, s32[1,5]{1,0:T(1,128)}, u32[]{:S(2)}) copy-start(s32[1,5]{1,0:T(1,128)} %param.7) | copy-start | bytes 64
  1.5 1.2 %copy-start = (bf16[512,1024]{1,0:T(8,128)(2,1)S(1)}, bf16[512,1024]{1,0:T(8,128)(2,1)}, u32[]{:S(2)}) copy-start(bf16[512,1024]{1,0:T(8,128)(2,1)} %x_ref.1) | copy-start | bytes 3145732
